TPU v7x, 32 devices: a whole 2x2x4 slice. The times are simulated.
32 devices in a mesh: slides: 2 (over y), seq: 16 (over z, x, core), mp: 1.
Axes of the slice: x: 2, y: 2, z: 4, core: 2. Of those that a mesh axis runs over, the one named last changes fastest.
Arguments:
- tokens: bfloat16 [32768, 768], P(('slides', 'seq', 'mp')), parts along dimension 0, may hold values from -6 to 6
- attn_gain: float32 [768], replicated, may hold values from 0.25 to 1.75
- query_first: bfloat16 [768, 768], P(None, 'mp'), may hold values from -4 to 4
- key_first: bfloat16 [768, 768], P(None, 'mp'), may hold values from -4 to 4
- segment_value: bfloat16 [768, 768], P(None, 'mp'), may hold values from -0.21875 to 0.21875
- output_first: bfloat16 [768, 768], P('mp'), may hold values from -0.875 to 0.875
- mlp_gain: float32 [768], replicated, may hold values from 0.25 to 1.75
- up_weight: bfloat16 [768, 3072], P(None, 'mp'), may hold values from -0.21875 to 0.21875
- down_weight: bfloat16 [3072, 768], P('mp'), may hold values from -0.109375 to 0.109375
- second_gain: float32 [768], replicated, may hold values from 0.25 to 1.75
- query_second: bfloat16 [768, 768], P(None, 'mp'), may hold values from -4 to 4
- key_second: bfloat16 [768, 768], P(None, 'mp'), may hold values from -4 to 4
- value_second: bfloat16 [768, 768], P(None, 'mp'), may hold values from -0.21875 to 0.21875
- output_second: bfloat16 [768, 768], P('mp'), may hold values from -0.875 to 0.875
- segment_offset: int32 [16], P('mp'), may hold values from 0 to 63
- global_offset: int32 [16], P('mp'), may hold values from 0 to 63
Outputs:
- encoded: bfloat16 [32768, 768], P(('slides', 'seq', 'mp')), parts along dimension 0
There are 2 independent parts, one for each index of `slides`. A program takes and returns all parts, laid end to end along the dimension named above; an argument that names none is the same for every part. Nothing has to cross between parts.
All inputs are finite; a program needn't handle non-finite values.
Results may differ from a plain program's by a relative error of at most 0.03.
The roundings to bfloat16 on the way count: a program that leaves them out, or rounds other values in their place, can miss the bound.
Values may be sent and summed in bfloat16 or wider, within the bound.
A program may use at most 128 MiB of HBM per device.

v0:
```python
import jax
import jax.numpy as jnp
from jax import lax
from jax.sharding import PartitionSpec as P

KEYS = 256
SEG_MAX = 16


def swapped(x, axis, apart):
    return lax.ppermute(x, axis, [(i, i ^ 1 << apart) for i in range(lax.axis_size(axis))])


def norm_rows(values, gain):
    center = values - jnp.mean(values, axis=-1, keepdims=True)
    spread = jnp.mean(center * center, axis=-1, keepdims=True)
    return (center * lax.rsqrt(spread + 1e-05) * gain).astype(jnp.bfloat16)


def pick_keys(hidden, offsets, stride, key_weight, value_weight):
    token_count, width = hidden.shape
    head_count = offsets.shape[0]
    head_size = key_weight.shape[1] // head_count
    grouped_rows = hidden.reshape(token_count // stride, stride, width)
    dilation_selector = (
        lax.broadcasted_iota(jnp.int32, (stride, head_count), 0) == offsets[None, :]
    ).astype(jnp.bfloat16)
    chosen = jnp.einsum(
        "nof,oj->njf", grouped_rows, dilation_selector, preferred_element_type=jnp.float32
    ).astype(jnp.bfloat16)
    key_heads = jnp.einsum(
        "xkr,rkf->xkf",
        chosen,
        key_weight.reshape(width, head_count, head_size),
        preferred_element_type=jnp.float32,
    ).astype(jnp.bfloat16)
    value_heads = jnp.einsum(
        "xkr,rkf->xkf",
        chosen,
        value_weight.reshape(width, head_count, head_size),
        preferred_element_type=jnp.float32,
    ).astype(jnp.bfloat16)
    picked = token_count // stride
    return jnp.stack(
        [
            key_heads.reshape(picked, head_count * head_size),
            value_heads.reshape(picked, head_count * head_size),
        ]
    )


def attend_local(query, keyval, head_count):
    token_count, width = query.shape
    head_size = width // head_count
    query_heads = query.reshape(token_count, head_count, head_size)
    key_heads = keyval[0].reshape(-1, head_count, head_size)
    value_heads = keyval[1].reshape(-1, head_count, head_size)
    scores = jnp.einsum(
        "thd,khd->htk", query_heads, key_heads, preferred_element_type=jnp.float32
    ) * head_size ** (-0.5)
    highest = jnp.max(scores, axis=-1, keepdims=True)
    weights = jnp.exp(scores - highest)
    weights = (weights / jnp.sum(weights, axis=-1, keepdims=True)).astype(jnp.bfloat16)
    mixed = jnp.einsum(
        "htk,khd->thd", weights, value_heads, preferred_element_type=jnp.float32
    ).astype(jnp.bfloat16)
    return mixed.reshape(token_count, width)


def merge_branch_pair(mine, other, level, token_position):
    lower = token_position >> level & 1 == 0
    return jnp.where(
        lower, jnp.concatenate((mine, other), axis=1), jnp.concatenate((other, mine), axis=1)
    )


def spread_segment(keyval, seg_span, token_position):
    for level in range(seg_span.bit_length() - 1):
        partner = swapped(keyval, "seq", level)
        keyval = merge_branch_pair(keyval, partner, level, token_position)
    return keyval


def spread_global(keyval_two):
    keyval_two = lax.all_gather(keyval_two, "seq", axis=1, tiled=True)
    return keyval_two


def combine(partial_value, residual_full, need_full):
    row_count = residual_full.shape[0] // lax.axis_size("mp")
    row_start = lax.axis_index("mp") * row_count
    share = lax.psum_scatter(partial_value, "mp", scatter_dimension=0, tiled=True)
    own_rows = lax.dynamic_slice_in_dim(residual_full, row_start, row_count, 0)
    own_rows = (own_rows.astype(jnp.float32) + share).astype(jnp.bfloat16)
    full_rows = lax.all_gather(own_rows, "mp", axis=0, tiled=True) if need_full else own_rows
    return (own_rows, full_rows)


def body(
    tokens,
    attn_gain,
    query_first,
    key_first,
    segment_value,
    output_first,
    mlp_gain,
    up_weight,
    down_weight,
    second_gain,
    query_second,
    key_second,
    value_second,
    output_second,
    segment_offset,
    global_offset,
):
    seq_count = lax.axis_size("seq")
    token_position = lax.axis_index("seq")
    seg_span = min(SEG_MAX, seq_count)
    head_count = segment_offset.shape[0]
    full_rows = lax.all_gather(tokens, "mp", axis=0, tiled=True)
    token_count = full_rows.shape[0]
    hidden = norm_rows(full_rows.astype(jnp.float32), attn_gain)
    query = jnp.dot(hidden, query_first, preferred_element_type=jnp.float32).astype(jnp.bfloat16)
    seg_stride = token_count // (KEYS // seg_span)
    keyval = pick_keys(hidden, segment_offset, seg_stride, key_first, segment_value)
    keyval = spread_segment(keyval, seg_span, token_position)
    mixed = attend_local(query, keyval, head_count)
    partial_value = jnp.dot(mixed, output_first, preferred_element_type=jnp.float32)
    own_rows, first_rows = combine(partial_value, full_rows, True)
    normed = norm_rows(first_rows.astype(jnp.float32), mlp_gain)
    inner = jax.nn.gelu(
        jnp.dot(normed, up_weight, preferred_element_type=jnp.float32), approximate=True
    ).astype(jnp.bfloat16)
    partial_value = jnp.dot(inner, down_weight, preferred_element_type=jnp.float32)
    own_rows, second_rows = combine(partial_value, first_rows, True)
    hidden_two = norm_rows(second_rows.astype(jnp.float32), second_gain)
    query_two = jnp.dot(hidden_two, query_second, preferred_element_type=jnp.float32).astype(
        jnp.bfloat16
    )
    glob_stride = token_count // (KEYS // seq_count)
    keyval_two = pick_keys(hidden_two, global_offset, glob_stride, key_second, value_second)
    keyval_two = spread_global(keyval_two)
    mixed_two = attend_local(query_two, keyval_two, head_count)
    partial_value = jnp.dot(mixed_two, output_second, preferred_element_type=jnp.float32)
    own_rows, unused_rows = combine(partial_value, second_rows, False)
    return own_rows


def solution(mesh):
    placed = (
        P(("slides", "seq", "mp"), None),
        P(),
        P(None, "mp"),
        P(None, "mp"),
        P(None, "mp"),
        P("mp", None),
        P(),
        P(None, "mp"),
        P("mp", None),
        P(),
        P(None, "mp"),
        P(None, "mp"),
        P(None, "mp"),
        P("mp", None),
        P("mp"),
        P("mp"),
    )
    return jax.shard_map(
        body,
        mesh=mesh,
        in_specs=placed,
        out_specs=P(("slides", "seq", "mp"), None),
        check_vma=False,
    )
```

profile of v0, /device:TPU:0, one launch (start us, length us, event | category | flops | bytes accessed | tf_op | source)
XLA Modules:
  0.0 132.9 jit_solution(15052510869012871012)
XLA Ops:
  0.0 2.5 %copy.27 = bf16[768,768]{0,1:T(8,128)(2,1)} copy(bf16[768,768]{1,0:T(8,128)(2,1)} %param.19) | data formatting | bytes 2359296 | tf_op args[3]
  2.5 0.3 convert_reduce_fusion.2
  2.8 0.6 fusion.34
  3.5 0.5 fusion.36
  4.0 1.1 copy-done.3
  5.1 0.4 fusion.60
  5.5 0.4 fusion.62
  6.0 0.1 stack_reshape.12
  6.1 2.4 %copy.30 = bf16[768,768]{0,1:T(8,128)(2,1)} copy(bf16[768,768]{1,0:T(8,128)(2,1)} %param.20) | data formatting | bytes 2359296 | tf_op args[4]
  8.5 1.7 %fusion.63 = bf16[16,16,48]{2,0,1:T(8,128)(2,1)S(1)} fusion(bf16[768,16,48]{0,2,1:T(8,128)(2,1)} %bitcast.67, bf16[16,16,768]{2,1,0:T(8,128)(2,1)S(1)} %fusion.60), kind=kOutput, calls=%fused_computation.70 | convolution fusion | flops 18886656 | bytes 1597440 | tf_op jit(solution)/shard_map/xkr,rkf->xkf/dot_general | solution.py:37
  10.2 0.1 stack_reshape.13
  10.3 0.6 collective-permute-start
  10.9 0.9 collective-permute-done
  11.8 2.9 %collective-permute-start.1 = (bf16[2,32,768]{2,1,0:T(8,128)(2,1)S(1)}, bf16[2,32,768]{2,1,0:T(8,128)(2,1)S(1)}, u32[]{:S(2)}, u32[]{:S(2)}) collective-permute-start(bf16[2,32,768]{2,1,0:T(8,128)(2,1)S(1)} %maximum_select_fusion.3), channel_id=1, source_target_pairs={{0,2},{1,3},{2,0},{3,1},{4,6},{5,7},{6,4},{7,5},{8,10},{9,11},{10,... | collective-permute-start | bytes 294920 | tf_op jit(solution)/shard_map/ppermute | solution.py:11
  14.7 3.1 %collective-permute-done.1 = bf16[2,32,768]{2,1,0:T(8,128)(2,1)S(1)} collective-permute-done((bf16[2,32,768]{2,1,0:T(8,128)(2,1)S(1)}, bf16[2,32,768]{2,1,0:T(8,128)(2,1)S(1)}, u32[]{:S(2)}, u32[]{:S(2)}) %collective-permute-start.1) | collective-permute-done | bytes 98336 | tf_op jit(solution)/shard_map/ppermute | solution.py:11
  17.9 1.9 %collective-permute-start.2 = (bf16[2,64,768]{2,1,0:T(8,128)(2,1)S(1)}, bf16[2,64,768]{2,1,0:T(8,128)(2,1)S(1)}, u32[]{:S(2)}, u32[]{:S(2)}) collective-permute-start(bf16[2,64,768]{2,1,0:T(8,128)(2,1)S(1)} %maximum_select_fusion.2), channel_id=1, source_target_pairs={{0,4},{1,5},{2,6},{3,7},{4,0},{5,1},{6,2},{7,3},{8,12},{9,13},{10,... | collective-permute-start | bytes 589832 | tf_op jit(solution)/shard_map/ppermute | solution.py:11
  19.8 4.6 %collective-permute-done.2 = bf16[2,64,768]{2,1,0:T(8,128)(2,1)S(1)} collective-permute-done((bf16[2,64,768]{2,1,0:T(8,128)(2,1)S(1)}, bf16[2,64,768]{2,1,0:T(8,128)(2,1)S(1)}, u32[]{:S(2)}, u32[]{:S(2)}) %collective-permute-start.2) | collective-permute-done | bytes 196640 | tf_op jit(solution)/shard_map/ppermute | solution.py:11
  24.3 0.1 maximum_select_fusion.1
  24.4 2.6 %collective-permute-start.3 = (bf16[2,128,768]{2,1,0:T(8,128)(2,1)S(1)}, bf16[2,128,768]{2,1,0:T(8,128)(2,1)S(1)}, u32[]{:S(2)}, u32[]{:S(2)}) collective-permute-start(bf16[2,128,768]{2,1,0:T(8,128)(2,1)S(1)} %maximum_select_fusion.1), channel_id=1, source_target_pairs={{0,8},{1,9},{2,10},{3,11},{4,12},{5,13},{6,14},{7,15},{8,0},{9,1},... | collective-permute-start | bytes 1179656 | tf_op jit(solution)/shard_map/ppermute | solution.py:11
  27.0 2.4 %copy.39 = bf16[768,768]{0,1:T(8,128)(2,1)} copy(bf16[768,768]{1,0:T(8,128)(2,1)} %param.28) | data formatting | bytes 2359296 | tf_op args[12]
  29.4 2.4 %copy.36 = bf16[768,768]{0,1:T(8,128)(2,1)} copy(bf16[768,768]{1,0:T(8,128)(2,1)} %param.27) | data formatting | bytes 2359296 | tf_op args[11]
  31.8 4.3 %convolution_convert_fusion.1 = bf16[1024,768]{0,1:T(8,128)(2,1)} fusion(bf16[1024,768]{1,0:T(8,128)(2,1)} %copy-done.3, bf16[768,768]{1,0:T(8,128)(2,1)} %param.18), kind=kOutput, calls=%fused_computation.57 | convolution fusion | flops 1208745984 | bytes 4325376 | tf_op jit(solution)/shard_map/dot_general | solution.py:124
  36.1 7.4 %collective-permute-done.3 = bf16[2,128,768]{2,1,0:T(8,128)(2,1)S(1)} collective-permute-done((bf16[2,128,768]{2,1,0:T(8,128)(2,1)S(1)}, bf16[2,128,768]{2,1,0:T(8,128)(2,1)S(1)}, u32[]{:S(2)}, u32[]{:S(2)}) %collective-permute-start.3) | collective-permute-done | bytes 393248 | tf_op jit(solution)/shard_map/ppermute | solution.py:11
  43.5 0.3 maximum_select_fusion
  43.8 0.1 fusion.83
  43.9 0.9 copy.33
  44.8 0.2 copy.34
  45.0 10.4 %fusion.84 = (f32[16,1024]{1,0:T(8,128)}, f32[16,1024,256]{1,2,0:T(8,128)}) fusion(bf16[1024,16,48]{0,2,1:T(8,128)(2,1)} %bitcast.72, bf16[256,16,48]{0,2,1:T(8,128)(2,1)S(1)} %bitcast.70), kind=kOutput, calls=%fused_computation.104 | convolution fusion | flops 415236352 | bytes 18808832 | tf_op jit(solution)/shard_map/sub | solution.py:62
  55.4 7.3 %fusion.47 = bf16[16,48,1024]{2,1,0:T(8,128)(2,1)S(1)} fusion(bf16[256,16,48]{0,2,1:T(8,128)(2,1)S(1)} %bitcast.69, f32[16,1024,256]{1,2,0:T(8,128)} %get-tuple-element.10, f32[16,1024]{1,0:T(8,128)} %get-tuple-element.9), kind=kOutput, calls=%fused_computation.55 | convolution fusion | flops 411828224 | bytes 18808832 | tf_op jit(solution)/shard_map/htk,khd->thd/dot_general | solution.py:64
  62.8 1.6 %convert_reduce_fusion.1 = (f32[1024]{0:T(1024)S(1)}, bf16[1024,768]{1,0:T(8,128)(2,1)S(1)}) fusion(bf16[1024,768]{0,1:T(8,128)(2,1)S(1)} %bitcast.74, bf16[768,768]{1,0:T(8,128)(2,1)S(1)} %copy-done, bf16[1024,768]{1,0:T(8,128)(2,1)S(1)} %copy-done.2), kind=kOutput, calls=%fused_computation.29 | convolution fusion | flops 1211890688 | bytes 5902336 | tf_op jit(solution)/shard_map/dot_general | solution.py:129
  64.3 0.6 fusion.31
  65.0 0.5 copy-done.8
  65.5 15.5 %convert_reduce_fusion = (f32[1024]{0:T(1024)S(1)}, bf16[1024,768]{1,0:T(8,128)(2,1)S(1)}) fusion(bf16[3072,768]{1,0:T(8,128)(2,1)} %param.24, bf16[768,3072]{1,0:T(8,128)(2,1)} %param.23, bf16[1024,768]{1,0:T(8,128)(2,1)} %copy-done.8, f32[768]{0:T(1024)S(1)} %copy-done.15, f32[1024]{0:T(1024)S(1)} %add_rsqrt_fusion.1, f32[1024]{0:T(1024)S(1)} %broadcast_multiply_fusion.1), kind=kOutput, calls=%fused_computation.26 | convolution fusion | flops 9699851264 | bytes 12598272 | tf_op jit(solution)/shard_map/dot_general | solution.py:135
  81.0 0.6 fusion.28
  81.6 0.5 fusion.30
  82.2 1.1 copy-done.4
  83.3 0.4 fusion.61
  83.7 0.4 fusion.65
  84.2 0.1 stack_reshape.15
  84.3 0.4 fusion.64
  84.7 0.1 stack_reshape.14
  84.9 23.6 %all_gather.2 = bf16[2,256,768]{2,1,0:T(8,128)(2,1)S(1)} all-gather(bf16[2,16,768]{2,1,0:T(8,128)(2,1)S(1)} %pad_maximum_fusion), channel_id=1, replica_groups=mesh['slides'=2,'seq'=16,'mp'=1] {'seq'}, dimensions={1}, use_global_device_ids=true | all-gather | bytes 835584 | tf_op jit(solution)/shard_map/all_gather | solution.py:85
  108.5 0.2 copy.42
  108.7 4.3 %convolution_convert_fusion = bf16[1024,768]{0,1:T(8,128)(2,1)} fusion(bf16[1024,768]{1,0:T(8,128)(2,1)} %copy-done.4, bf16[768,768]{1,0:T(8,128)(2,1)} %param.26), kind=kOutput, calls=%fused_computation.56 | convolution fusion | flops 1208745984 | bytes 4325376 | tf_op jit(solution)/shard_map/dot_general | solution.py:138
  113.0 0.2 copy.43
  113.2 9.7 %fusion.87 = (f32[16,1024]{1,0:T(8,128)S(1)}, f32[16,1024,256]{1,2,0:T(8,128)}) fusion(bf16[1024,16,48]{0,2,1:T(8,128)(2,1)} %bitcast.73, bf16[256,16,48]{0,2,1:T(8,128)(2,1)S(1)} %bitcast.71), kind=kOutput, calls=%fused_computation.105 | convolution fusion | flops 415236352 | bytes 18808832 | tf_op jit(solution)/shard_map/sub | solution.py:62
  122.9 7.4 %fusion.46 = bf16[16,48,1024]{2,1,0:T(8,128)(2,1)S(1)} fusion(bf16[256,16,48]{0,2,1:T(8,128)(2,1)S(1)} %bitcast.68, f32[16,1024,256]{1,2,0:T(8,128)} %get-tuple-element.16, f32[16,1024]{1,0:T(8,128)S(1)} %get-tuple-element.15), kind=kOutput, calls=%fused_computation.54 | convolution fusion | flops 411828224 | bytes 18808832 | tf_op jit(solution)/shard_map/htk,khd->thd/dot_general | solution.py:64
  130.4 2.6 %fusion.39 = bf16[1024,768]{1,0:T(8,128)(2,1)} fusion(bf16[1024,768]{1,0:T(8,128)(2,1)S(1)} %get-tuple-element.14, bf16[1024,768]{0,1:T(8,128)(2,1)S(1)} %bitcast.75, bf16[768,768]{1,0:T(8,128)(2,1)S(1)} %copy-done.14), kind=kOutput, calls=%fused_computation.50 | convolution fusion | flops 1210318848 | bytes 5898240 | tf_op jit(solution)/shard_map/dot_general | solution.py:145
  (45 shorter events, 0.4 us)
Async XLA Ops:
  0.0 62.7 %copy-start = (bf16[768,768]{1,0:T(8,128)(2,1)S(1)}, bf16[768,768]{1,0:T(8,128)(2,1)}, u32[]{:S(2)}) copy-start(bf16[768,768]{1,0:T(8,128)(2,1)} %param.21) | copy-start | bytes 3538948
  0.0 2.5 %copy-start.2 = (bf16[1024,768]{1,0:T(8,128)(2,1)S(1)}, bf16[1024,768]{1,0:T(8,128)(2,1)}, u32[]{:S(2)}) copy-start(bf16[1024,768]{1,0:T(8,128)(2,1)} %param.16) | copy-start | bytes 4718596
  0.0 3.4 %copy-start.10 = (f32[768]{0:T(1024)S(1)}, f32[768]{0:T(1024)}, u32[]{:S(2)}) copy-start(f32[768]{0:T(1024)} %param.17) | copy-start | bytes 9220
  2.5 2.6 %copy-start.12 = (s32[16]{0:T(128)S(1)}, s32[16]{0:T(128)}, u32[]{:S(2)}) copy-start(s32[16]{0:T(128)} %param.30) | copy-start | bytes 196
  2.8 2.7 %copy-start.7 = (bf16[768,768]{0,1:T(8,128)(2,1)S(1)}, bf16[768,768]{0,1:T(8,128)(2,1)}, u32[]{:S(2)}) copy-start(bf16[768,768]{0,1:T(8,128)(2,1)} %copy.27) | copy-start | bytes 3538948
  4.0 1.1 copy-start.3
  10.3 1.4 %collective-permute-start = (bf16[2,16,768]{2,1,0:T(8,128)(2,1)S(1)}, bf16[2,16,768]{2,1,0:T(8,128)(2,1)S(1)}, u32[]{:S(2)}, u32[]{:S(2)}) collective-permute-start(bf16[2,16,768]{2,1,0:T(8,128)(2,1)S(1)} %constant_dynamic-update-slice_fusion), channel_id=1, source_target_pairs={{0,1},{1,0},{2,3},{3,2},{4,5},{5,4},{6,7},{7,6},{8,9},{9,8},{10,11... | collective-permute-start | bytes 147464 | tf_op jit(solution)/shard_map/ppermute | solution.py:11
  11.8 6.0 %collective-permute-start.1 = (bf16[2,32,768]{2,1,0:T(8,128)(2,1)S(1)}, bf16[2,32,768]{2,1,0:T(8,128)(2,1)S(1)}, u32[]{:S(2)}, u32[]{:S(2)}) collective-permute-start(bf16[2,32,768]{2,1,0:T(8,128)(2,1)S(1)} %maximum_select_fusion.3), channel_id=1, source_target_pairs={{0,2},{1,3},{2,0},{3,1},{4,6},{5,7},{6,4},{7,5},{8,10},{9,11},{10,... | collective-permute-start | bytes 294920 | tf_op jit(solution)/shard_map/ppermute | solution.py:11
  17.9 6.5 %collective-permute-start.2 = (bf16[2,64,768]{2,1,0:T(8,128)(2,1)S(1)}, bf16[2,64,768]{2,1,0:T(8,128)(2,1)S(1)}, u32[]{:S(2)}, u32[]{:S(2)}) collective-permute-start(bf16[2,64,768]{2,1,0:T(8,128)(2,1)S(1)} %maximum_select_fusion.2), channel_id=1, source_target_pairs={{0,4},{1,5},{2,6},{3,7},{4,0},{5,1},{6,2},{7,3},{8,12},{9,13},{10,... | collective-permute-start | bytes 589832 | tf_op jit(solution)/shard_map/ppermute | solution.py:11
  24.4 19.1 %collective-permute-start.3 = (bf16[2,128,768]{2,1,0:T(8,128)(2,1)S(1)}, bf16[2,128,768]{2,1,0:T(8,128)(2,1)S(1)}, u32[]{:S(2)}, u32[]{:S(2)}) collective-permute-start(bf16[2,128,768]{2,1,0:T(8,128)(2,1)S(1)} %maximum_select_fusion.1), channel_id=1, source_target_pairs={{0,8},{1,9},{2,10},{3,11},{4,12},{5,13},{6,14},{7,15},{8,0},{9,1},... | collective-permute-start | bytes 1179656 | tf_op jit(solution)/shard_map/ppermute | solution.py:11
  45.0 10.4 %copy-start.9 = (bf16[1,256,768]{1,2,0:T(8,128)(2,1)S(1)}, bf16[1,256,768]{1,2,0:T(8,128)(2,1)}, u32[]{:S(2)}) copy-start(bf16[1,256,768]{1,2,0:T(8,128)(2,1)} %copy.33) | copy-start | bytes 1179652
  62.7 2.7 %copy-start.15 = (f32[768]{0:T(1024)S(1)}, f32[768]{0:T(1024)}, u32[]{:S(2)}) copy-start(f32[768]{0:T(1024)} %param.22) | copy-start | bytes 9220
  64.3 1.1 copy-start.8
  65.5 16.1 %copy-start.11 = (f32[768]{0:T(1024)S(1)}, f32[768]{0:T(1024)}, u32[]{:S(2)}) copy-start(f32[768]{0:T(1024)} %param.25) | copy-start | bytes 9220
  81.0 2.4 %copy-start.13 = (s32[16]{0:T(128)S(1)}, s32[16]{0:T(128)}, u32[]{:S(2)}) copy-start(s32[16]{0:T(128)} %param.31) | copy-start | bytes 196
  81.0 2.7 %copy-start.6 = (bf16[768,768]{0,1:T(8,128)(2,1)S(1)}, bf16[768,768]{0,1:T(8,128)(2,1)}, u32[]{:S(2)}) copy-start(bf16[768,768]{0,1:T(8,128)(2,1)} %copy.39) | copy-start | bytes 3538948
  81.6 2.7 %copy-start.5 = (bf16[768,768]{0,1:T(8,128)(2,1)S(1)}, bf16[768,768]{0,1:T(8,128)(2,1)}, u32[]{:S(2)}) copy-start(bf16[768,768]{0,1:T(8,128)(2,1)} %copy.36) | copy-start | bytes 3538948
  82.2 1.1 copy-start.4
  122.9 7.5 %copy-start.14 = (bf16[768,768]{1,0:T(8,128)(2,1)S(1)}, bf16[768,768]{1,0:T(8,128)(2,1)}, u32[]{:S(2)}) copy-start(bf16[768,768]{1,0:T(8,128)(2,1)} %param.29) | copy-start | bytes 3538948
  130.3 2.6 %copy-start.1 = (bf16[768,768]{1,0:T(8,128)(2,1)S(1)}, bf16[768,768]{1,0:T(8,128)(2,1)}, u32[]{:S(2)}) copy-start(bf16[768,768]{1,0:T(8,128)(2,1)} %param.21) | copy-start | bytes 3538948
where the time goes:
time: 133 us
  matrix products  66.8 us (50%)
  blocking collectives  23.6 us (18%)
  waiting for transfers between devices  16 us (12%)
  local copies, waits for them, and re-layouts  14.6 us (11%)
  starting transfers between devices  7.97 us (6%)
  other arithmetic  3.63 us (3%)
    all_gather x1, blocking collectives, spread_global(): keyval_two = lax.all_gather(keyval_two, 'seq', axis=1, tiled=True)  23.6 us
    sub x2, matrix products, attend_local(): weights = jnp.exp(scores - highest)  20.1 us
    ppermute x4, waiting for transfers between devices, swapped(): lax.ppermute(x, axis, [(i, i ^ 1 << apart) for i in range(lax.axis_size(a...  16 us
    dot_general x1, matrix products, body(): jnp.dot(inner, down_weight, preferred_element_type=jnp.float32)  15.5 us
    dot_general x2, matrix products, attend_local(): jnp.einsum('htk,khd->thd', weights, value_heads, preferred_element_type=j...  14.8 us
    unnamed x37, local copies, waits for them, and re-layouts  12.5 us
    ppermute x4, starting transfers between devices, swapped(): lax.ppermute(x, axis, [(i, i ^ 1 << apart) for i in range(lax.axis_size(a...  7.97 us
    dot_general x1, matrix products, body(): jnp.dot(hidden_two, query_second, preferred_element_type=jnp.float32)  4.34 us
  transfers between devices with their start and end apart: 4, of which 4 were waited for; matrix products, arithmetic and copies ran while one was open for 7% of the time, Pallas kernels for 0%

commit v1 on v0

--- a/solution.py
+++ b/solution.py
@@ -5,6 +5,27 @@
 
 KEYS = 256
 SEG_MAX = 16
+
+
+def joined_along(parts, dim):
+    parts = jnp.moveaxis(parts, 0, dim)
+    dims = parts.shape
+    return parts.reshape(*dims[:dim], dims[dim] * dims[dim + 1], *dims[dim + 2 :])
+
+
+def grow_blocks(array, axis):
+    length, here = (lax.axis_size(axis), lax.axis_index(axis))
+    blocks, apart = (array[None], 1)
+    while apart < length:
+        theirs = lax.ppermute(blocks, axis, [(i, i ^ apart) for i in range(length)])
+        low = here & apart == 0
+        blocks = jnp.concatenate([jnp.where(low, blocks, theirs), jnp.where(low, theirs, blocks)])
+        apart *= 2
+    return blocks
+
+
+def gather_by_bits(shard, axis, dim):
+    return joined_along(grow_blocks(shard, axis), dim)
 
 
 def swapped(x, axis, apart):
@@ -82,7 +103,7 @@
 
 
 def spread_global(keyval_two):
-    keyval_two = lax.all_gather(keyval_two, "seq", axis=1, tiled=True)
+    keyval_two = gather_by_bits(keyval_two, "seq", 1)
     return keyval_two
 
 

time: 133 us -> 144 us (1.083)
  blocking collectives: 23.6 us -> 0 us
  waiting for transfers between devices: 16 us -> 39.1 us
  local copies, waits for them, and re-layouts: 14.6 us -> 18.6 us
  starting transfers between devices: 7.97 us -> 11.8 us
  other arithmetic: 3.63 us -> 6.86 us
    all_gather x1 -> x0, blocking collectives: 23.6 us -> none  [spread_global(): keyval_two = lax.all_gather(keyval_two, 'seq', axis=1, tiled=True)]
    ppermute x0 -> x4, waiting for transfers between devices: none -> 23.1 us  [grow_blocks(): theirs = lax.ppermute(blocks, axis, [(i, i ^ apart) for i in range(length)])]
    another operation x0 -> x2, local copies, waits for them, and re-layouts: none -> 4.39 us  [the longest x1 2.2 us: attend_local(): key_heads = keyval[0].reshape(-1, head_count, head_size)]
    ppermute x0 -> x4, starting transfers between devices: none -> 3.81 us  [grow_blocks(): theirs = lax.ppermute(blocks, axis, [(i, i ^ apart) for i in range(length)])]
    reduce_sum x1, other arithmetic: 0.27 us -> 1.83 us  [norm_rows(): center = values - jnp.mean(values, axis=-1, keepdims=True)]
  transfers between devices with their start and end apart: 4 -> 8, of which waited for: 4 -> 8; matrix products, arithmetic and copies ran while one was open for 7% -> 9% of each run, Pallas kernels for 0% -> 0%
where the time goes in v1:
time: 144 us
  matrix products  67.1 us (47%)
  waiting for transfers between devices  39.1 us (27%)
  local copies, waits for them, and re-layouts  18.6 us (13%)
  starting transfers between devices  11.8 us (8%)
  other arithmetic  6.86 us (5%)
    ppermute x4, waiting for transfers between devices, grow_blocks(): theirs = lax.ppermute(blocks, axis, [(i, i ^ apart) for i in range(length)])  23.1 us
    sub x2, matrix products, attend_local(): weights = jnp.exp(scores - highest)  20 us
    ppermute x4, waiting for transfers between devices, swapped(): lax.ppermute(x, axis, [(i, i ^ 1 << apart) for i in range(lax.axis_size(a...  16 us
    dot_general x1, matrix products, body(): jnp.dot(inner, down_weight, preferred_element_type=jnp.float32)  15.5 us
    dot_general x2, matrix products, attend_local(): jnp.einsum('htk,khd->thd', weights, value_heads, preferred_element_type=j...  15.1 us
    unnamed x37, local copies, waits for them, and re-layouts  12.4 us
    ppermute x4, starting transfers between devices, swapped(): lax.ppermute(x, axis, [(i, i ^ 1 << apart) for i in range(lax.axis_size(a...  7.97 us
    dot_general x1, matrix products, body(): jnp.dot(hidden_two, query_second, preferred_element_type=jnp.float32)  4.35 us
  transfers between devices with their start and end apart: 8, of which 8 were waited for; matrix products, arithmetic and copies ran while one was open for 9% of the time, Pallas kernels for 0%

profile of v1, /device:TPU:0, one launch (start us, length us, event | category | flops | bytes accessed | tf_op | source)
XLA Modules:
  0.0 143.8 jit_solution(2183904460326714140)
XLA Ops:
  0.0 1.8 %convert_reduce_fusion.2 = f32[1024]{0:T(1024)S(1)} fusion(bf16[1024,768]{1,0:T(8,128)(2,1)} %param.16), kind=kLoop, calls=%fused_computation.32 | loop fusion | flops 1571840 | bytes 1576960 | tf_op jit(solution)/shard_map/reduce_sum | solution.py:36
  1.8 2.0 %fusion.34 = f32[1024]{0:T(1024)S(1)} fusion(bf16[1024,768]{1,0:T(8,128)(2,1)} %param.16, f32[1024]{0:T(1024)S(1)} %broadcast_multiply_fusion.2), kind=kLoop, calls=%fused_computation.45 | loop fusion | flops 3144704 | bytes 1581056 | tf_op jit(solution)/shard_map/reduce_sum | solution.py:37
  3.9 2.4 %copy.27 = bf16[768,768]{0,1:T(8,128)(2,1)} copy(bf16[768,768]{1,0:T(8,128)(2,1)} %param.19) | data formatting | bytes 2359296 | tf_op args[3]
  6.3 0.5 fusion.36
  6.8 1.1 copy-done.4
  8.0 0.4 fusion.60
  8.4 0.4 fusion.62
  9.0 2.4 %copy.30 = bf16[768,768]{0,1:T(8,128)(2,1)} copy(bf16[768,768]{1,0:T(8,128)(2,1)} %param.20) | data formatting | bytes 2359296 | tf_op args[4]
  11.4 1.7 %fusion.63 = bf16[16,16,48]{2,0,1:T(8,128)(2,1)S(1)} fusion(bf16[768,16,48]{0,2,1:T(8,128)(2,1)} %bitcast.78, bf16[16,16,768]{2,1,0:T(8,128)(2,1)S(1)} %fusion.60), kind=kOutput, calls=%fused_computation.70 | convolution fusion | flops 18886656 | bytes 1597440 | tf_op jit(solution)/shard_map/xkr,rkf->xkf/dot_general | solution.py:58
  13.2 0.6 collective-permute-start
  13.8 0.9 collective-permute-done
  14.7 2.9 %collective-permute-start.1 = (bf16[2,32,768]{2,1,0:T(8,128)(2,1)S(1)}, bf16[2,32,768]{2,1,0:T(8,128)(2,1)S(1)}, u32[]{:S(2)}, u32[]{:S(2)}) collective-permute-start(bf16[2,32,768]{2,1,0:T(8,128)(2,1)S(1)} %maximum_select_fusion.3), channel_id=1, source_target_pairs={{0,2},{1,3},{2,0},{3,1},{4,6},{5,7},{6,4},{7,5},{8,10},{9,11},{10,... | collective-permute-start | bytes 294920 | tf_op jit(solution)/shard_map/ppermute | solution.py:32
  17.6 3.1 %collective-permute-done.1 = bf16[2,32,768]{2,1,0:T(8,128)(2,1)S(1)} collective-permute-done((bf16[2,32,768]{2,1,0:T(8,128)(2,1)S(1)}, bf16[2,32,768]{2,1,0:T(8,128)(2,1)S(1)}, u32[]{:S(2)}, u32[]{:S(2)}) %collective-permute-start.1) | collective-permute-done | bytes 98336 | tf_op jit(solution)/shard_map/ppermute | solution.py:32
  20.7 1.9 %collective-permute-start.2 = (bf16[2,64,768]{2,1,0:T(8,128)(2,1)S(1)}, bf16[2,64,768]{2,1,0:T(8,128)(2,1)S(1)}, u32[]{:S(2)}, u32[]{:S(2)}) collective-permute-start(bf16[2,64,768]{2,1,0:T(8,128)(2,1)S(1)} %maximum_select_fusion.2), channel_id=1, source_target_pairs={{0,4},{1,5},{2,6},{3,7},{4,0},{5,1},{6,2},{7,3},{8,12},{9,13},{10,... | collective-permute-start | bytes 589832 | tf_op jit(solution)/shard_map/ppermute | solution.py:32
  22.6 4.6 %collective-permute-done.2 = bf16[2,64,768]{2,1,0:T(8,128)(2,1)S(1)} collective-permute-done((bf16[2,64,768]{2,1,0:T(8,128)(2,1)S(1)}, bf16[2,64,768]{2,1,0:T(8,128)(2,1)S(1)}, u32[]{:S(2)}, u32[]{:S(2)}) %collective-permute-start.2) | collective-permute-done | bytes 196640 | tf_op jit(solution)/shard_map/ppermute | solution.py:32
  27.3 2.6 %collective-permute-start.3 = (bf16[2,128,768]{2,1,0:T(8,128)(2,1)S(1)}, bf16[2,128,768]{2,1,0:T(8,128)(2,1)S(1)}, u32[]{:S(2)}, u32[]{:S(2)}) collective-permute-start(bf16[2,128,768]{2,1,0:T(8,128)(2,1)S(1)} %maximum_select_fusion.1), channel_id=1, source_target_pairs={{0,8},{1,9},{2,10},{3,11},{4,12},{5,13},{6,14},{7,15},{8,0},{9,1},... | collective-permute-start | bytes 1179656 | tf_op jit(solution)/shard_map/ppermute | solution.py:32
  29.9 2.4 %copy.36 = bf16[768,768]{0,1:T(8,128)(2,1)} copy(bf16[768,768]{1,0:T(8,128)(2,1)} %param.27) | data formatting | bytes 2359296 | tf_op args[11]
  32.3 2.4 %copy.39 = bf16[768,768]{0,1:T(8,128)(2,1)} copy(bf16[768,768]{1,0:T(8,128)(2,1)} %param.28) | data formatting | bytes 2359296 | tf_op args[12]
  34.6 4.3 %convolution_convert_fusion.1 = bf16[1024,768]{0,1:T(8,128)(2,1)} fusion(bf16[1024,768]{1,0:T(8,128)(2,1)} %copy-done.4, bf16[768,768]{1,0:T(8,128)(2,1)} %param.18), kind=kOutput, calls=%fused_computation.57 | convolution fusion | flops 1208745984 | bytes 4325376 | tf_op jit(solution)/shard_map/dot_general | solution.py:145
  39.0 7.4 %collective-permute-done.3 = bf16[2,128,768]{2,1,0:T(8,128)(2,1)S(1)} collective-permute-done((bf16[2,128,768]{2,1,0:T(8,128)(2,1)S(1)}, bf16[2,128,768]{2,1,0:T(8,128)(2,1)S(1)}, u32[]{:S(2)}, u32[]{:S(2)}) %collective-permute-start.3) | collective-permute-done | bytes 393248 | tf_op jit(solution)/shard_map/ppermute | solution.py:32
  46.4 0.3 maximum_select_fusion
  46.8 0.9 copy.34
  47.7 0.2 copy.33
  47.9 9.8 %fusion.92 = (f32[16,1024]{1,0:T(8,128)S(1)}, f32[16,1024,256]{1,2,0:T(8,128)}) fusion(bf16[1024,16,48]{0,2,1:T(8,128)(2,1)} %bitcast.82, bf16[256,16,48]{0,2,1:T(8,128)(2,1)} %bitcast.79), kind=kOutput, calls=%fused_computation.120 | convolution fusion | flops 415236352 | bytes 18808832 | tf_op jit(solution)/shard_map/sub | solution.py:83
  57.6 7.3 %fusion.46 = bf16[16,48,1024]{2,1,0:T(8,128)(2,1)S(1)} fusion(bf16[256,16,48]{0,2,1:T(8,128)(2,1)S(1)} %bitcast.80, f32[16,1024,256]{1,2,0:T(8,128)} %get-tuple-element.18, f32[16,1024]{1,0:T(8,128)S(1)} %get-tuple-element.17), kind=kOutput, calls=%fused_computation.54 | convolution fusion | flops 411828224 | bytes 18808832 | tf_op jit(solution)/shard_map/htk,khd->thd/dot_general | solution.py:85
  65.0 1.6 %convert_reduce_fusion.1 = (f32[1024]{0:T(1024)S(1)}, bf16[1024,768]{1,0:T(8,128)(2,1)S(1)}) fusion(bf16[1024,768]{0,1:T(8,128)(2,1)S(1)} %bitcast.83, bf16[768,768]{1,0:T(8,128)(2,1)S(1)} %copy-done, bf16[1024,768]{1,0:T(8,128)(2,1)S(1)} %copy-done.2), kind=kOutput, calls=%fused_computation.29 | convolution fusion | flops 1211890688 | bytes 5902336 | tf_op jit(solution)/shard_map/dot_general | solution.py:150
  66.6 0.6 fusion.31
  67.2 0.5 copy-done.8
  67.7 15.5 %convert_reduce_fusion = (f32[1024]{0:T(1024)S(1)}, bf16[1024,768]{1,0:T(8,128)(2,1)S(1)}) fusion(bf16[3072,768]{1,0:T(8,128)(2,1)} %param.24, bf16[768,3072]{1,0:T(8,128)(2,1)} %param.23, bf16[1024,768]{1,0:T(8,128)(2,1)} %copy-done.8, f32[768]{0:T(1024)S(1)} %copy-done.15, f32[1024]{0:T(1024)S(1)} %add_rsqrt_fusion.1, f32[1024]{0:T(1024)S(1)} %broadcast_multiply_fusion.1), kind=kOutput, calls=%fused_computation.26 | convolution fusion | flops 9699851264 | bytes 12598272 | tf_op jit(solution)/shard_map/dot_general | solution.py:156
  83.2 0.6 fusion.28
  83.9 0.5 fusion.30
  84.4 1.1 copy-done.3
  85.6 0.4 fusion.61
  85.9 0.4 fusion.64
  86.5 0.4 fusion.65
  87.2 1.2 collective-permute-done.4
  88.4 1.2 collective-permute-start.5
  89.7 3.7 %collective-permute-done.5 = bf16[2,2,16,768]{3,2,1,0:T(8,128)(2,1)S(1)} collective-permute-done((bf16[2,2,16,768]{3,2,1,0:T(8,128)(2,1)S(1)}, bf16[2,2,16,768]{3,2,1,0:T(8,128)(2,1)S(1)}, u32[]{:S(2)}, u32[]{:S(2)}) %collective-permute-start.5) | collective-permute-done | bytes 98336 | tf_op jit(solution)/shard_map/ppermute | solution.py:20
  93.4 0.4 collective-permute-start.6
  93.8 5.8 %collective-permute-done.6 = bf16[4,2,16,768]{3,2,1,0:T(8,128)(2,1)S(1)} collective-permute-done((bf16[4,2,16,768]{3,2,1,0:T(8,128)(2,1)S(1)}, bf16[4,2,16,768]{3,2,1,0:T(8,128)(2,1)S(1)}, u32[]{:S(2)}, u32[]{:S(2)}) %collective-permute-start.6) | collective-permute-done | bytes 196640 | tf_op jit(solution)/shard_map/ppermute | solution.py:20
  99.7 2.1 %collective-permute-start.7 = (bf16[8,2,16,768]{3,2,1,0:T(8,128)(2,1)S(1)}, bf16[8,2,16,768]{3,2,1,0:T(8,128)(2,1)S(1)}, u32[]{:S(2)}, u32[]{:S(2)}) collective-permute-start(bf16[8,2,16,768]{3,2,1,0:T(8,128)(2,1)S(1)} %pad_maximum_fusion), channel_id=1, source_target_pairs={{0,8},{1,9},{2,10},{3,11},{4,12},{5,13},{6,14},{7,15},{8,0},{9,1},... | collective-permute-start | bytes 1179656 | tf_op jit(solution)/shard_map/ppermute | solution.py:20
  101.8 4.3 %convolution_convert_fusion = bf16[1024,768]{0,1:T(8,128)(2,1)} fusion(bf16[1024,768]{1,0:T(8,128)(2,1)} %copy-done.3, bf16[768,768]{1,0:T(8,128)(2,1)} %param.26), kind=kOutput, calls=%fused_computation.56 | convolution fusion | flops 1208745984 | bytes 4325376 | tf_op jit(solution)/shard_map/dot_general | solution.py:159
  106.1 12.4 %collective-permute-done.7 = bf16[8,2,16,768]{3,2,1,0:T(8,128)(2,1)S(1)} collective-permute-done((bf16[8,2,16,768]{3,2,1,0:T(8,128)(2,1)S(1)}, bf16[8,2,16,768]{3,2,1,0:T(8,128)(2,1)S(1)}, u32[]{:S(2)}, u32[]{:S(2)}) %collective-permute-start.7) | collective-permute-done | bytes 393248 | tf_op jit(solution)/shard_map/ppermute | solution.py:20
  118.7 2.2 %reshape_squeeze.15 = bf16[256,16,48]{2,1,0:T(8,128)(2,1)} reshape(bf16[1,16,16,768]{3,2,0,1:T(8,128)(2,1)S(1)} %get-tuple-element.6) | data formatting | bytes 786432 | tf_op jit(solution)/shard_map/reshape;squeeze | solution.py:77
  120.9 2.2 %reshape_squeeze.14 = bf16[256,16,48]{2,1,0:T(8,128)(2,1)} reshape(bf16[1,16,16,768]{3,2,0,1:T(8,128)(2,1)S(1)} %get-tuple-element.5) | data formatting | bytes 786432 | tf_op jit(solution)/shard_map/reshape;squeeze | solution.py:78
  123.1 10.2 %fusion.95 = (f32[16,1024]{1,0:T(8,128)S(1)}, f32[16,1024,256]{1,2,0:T(8,128)}) fusion(bf16[1024,16,48]{0,2,1:T(8,128)(2,1)} %bitcast.81, bf16[256,16,48]{2,1,0:T(8,128)(2,1)} %reshape_squeeze.15), kind=kOutput, calls=%fused_computation.121 | convolution fusion | flops 415236352 | bytes 18808832 | tf_op jit(solution)/shard_map/sub | solution.py:83
  133.4 7.8 %fusion.47 = bf16[16,48,1024]{2,1,0:T(8,128)(2,1)S(1)} fusion(f32[16,1024,256]{1,2,0:T(8,128)} %get-tuple-element.24, f32[16,1024]{1,0:T(8,128)S(1)} %get-tuple-element.23, bf16[256,16,48]{2,1,0:T(8,128)(2,1)S(1)} %copy-done.9), kind=kOutput, calls=%fused_computation.55 | convolution fusion | flops 411828224 | bytes 18808832 | tf_op jit(solution)/shard_map/htk,khd->thd/dot_general | solution.py:85
  141.2 2.6 %fusion.39 = bf16[1024,768]{1,0:T(8,128)(2,1)} fusion(bf16[1024,768]{1,0:T(8,128)(2,1)S(1)} %get-tuple-element.22, bf16[1024,768]{0,1:T(8,128)(2,1)S(1)} %bitcast.84, bf16[768,768]{1,0:T(8,128)(2,1)S(1)} %copy-done.14), kind=kOutput, calls=%fused_computation.50 | convolution fusion | flops 1210318848 | bytes 5898240 | tf_op jit(solution)/shard_map/dot_general | solution.py:166
  (60 shorter events, 1.3 us)
Async XLA Ops:
  0.0 65.0 %copy-start = (bf16[768,768]{1,0:T(8,128)(2,1)S(1)}, bf16[768,768]{1,0:T(8,128)(2,1)}, u32[]{:S(2)}) copy-start(bf16[768,768]{1,0:T(8,128)(2,1)} %param.21) | copy-start | bytes 3538948
  0.0 6.3 %copy-start.2 = (bf16[1024,768]{1,0:T(8,128)(2,1)S(1)}, bf16[1024,768]{1,0:T(8,128)(2,1)}, u32[]{:S(2)}) copy-start(bf16[1024,768]{1,0:T(8,128)(2,1)} %param.16) | copy-start | bytes 4718596
  0.0 6.3 %copy-start.10 = (f32[768]{0:T(1024)S(1)}, f32[768]{0:T(1024)}, u32[]{:S(2)}) copy-start(f32[768]{0:T(1024)} %param.17) | copy-start | bytes 9220
  3.9 4.1 %copy-start.12 = (s32[16]{0:T(128)S(1)}, s32[16]{0:T(128)}, u32[]{:S(2)}) copy-start(s32[16]{0:T(128)} %param.30) | copy-start | bytes 196
  6.3 2.1 %copy-start.7 = (bf16[768,768]{0,1:T(8,128)(2,1)S(1)}, bf16[768,768]{0,1:T(8,128)(2,1)}, u32[]{:S(2)}) copy-start(bf16[768,768]{0,1:T(8,128)(2,1)} %copy.27) | copy-start | bytes 3538948
  6.8 1.1 copy-start.4
  13.2 1.4 %collective-permute-start = (bf16[2,16,768]{2,1,0:T(8,128)(2,1)S(1)}, bf16[2,16,768]{2,1,0:T(8,128)(2,1)S(1)}, u32[]{:S(2)}, u32[]{:S(2)}) collective-permute-start(bf16[2,16,768]{2,1,0:T(8,128)(2,1)S(1)} %constant_dynamic-update-slice_fusion), channel_id=1, source_target_pairs={{0,1},{1,0},{2,3},{3,2},{4,5},{5,4},{6,7},{7,6},{8,9},{9,8},{10,11... | collective-permute-start | bytes 147464 | tf_op jit(solution)/shard_map/ppermute | solution.py:32
  14.7 6.0 %collective-permute-start.1 = (bf16[2,32,768]{2,1,0:T(8,128)(2,1)S(1)}, bf16[2,32,768]{2,1,0:T(8,128)(2,1)S(1)}, u32[]{:S(2)}, u32[]{:S(2)}) collective-permute-start(bf16[2,32,768]{2,1,0:T(8,128)(2,1)S(1)} %maximum_select_fusion.3), channel_id=1, source_target_pairs={{0,2},{1,3},{2,0},{3,1},{4,6},{5,7},{6,4},{7,5},{8,10},{9,11},{10,... | collective-permute-start | bytes 294920 | tf_op jit(solution)/shard_map/ppermute | solution.py:32
  20.7 6.5 %collective-permute-start.2 = (bf16[2,64,768]{2,1,0:T(8,128)(2,1)S(1)}, bf16[2,64,768]{2,1,0:T(8,128)(2,1)S(1)}, u32[]{:S(2)}, u32[]{:S(2)}) collective-permute-start(bf16[2,64,768]{2,1,0:T(8,128)(2,1)S(1)} %maximum_select_fusion.2), channel_id=1, source_target_pairs={{0,4},{1,5},{2,6},{3,7},{4,0},{5,1},{6,2},{7,3},{8,12},{9,13},{10,... | collective-permute-start | bytes 589832 | tf_op jit(solution)/shard_map/ppermute | solution.py:32
  27.3 19.1 %collective-permute-start.3 = (bf16[2,128,768]{2,1,0:T(8,128)(2,1)S(1)}, bf16[2,128,768]{2,1,0:T(8,128)(2,1)S(1)}, u32[]{:S(2)}, u32[]{:S(2)}) collective-permute-start(bf16[2,128,768]{2,1,0:T(8,128)(2,1)S(1)} %maximum_select_fusion.1), channel_id=1, source_target_pairs={{0,8},{1,9},{2,10},{3,11},{4,12},{5,13},{6,14},{7,15},{8,0},{9,1},... | collective-permute-start | bytes 1179656 | tf_op jit(solution)/shard_map/ppermute | solution.py:32
  65.0 2.7 %copy-start.15 = (f32[768]{0:T(1024)S(1)}, f32[768]{0:T(1024)}, u32[]{:S(2)}) copy-start(f32[768]{0:T(1024)} %param.22) | copy-start | bytes 9220
  66.6 1.1 copy-start.8
  67.7 16.1 %copy-start.11 = (f32[768]{0:T(1024)S(1)}, f32[768]{0:T(1024)}, u32[]{:S(2)}) copy-start(f32[768]{0:T(1024)} %param.25) | copy-start | bytes 9220
  83.2 2.4 %copy-start.13 = (s32[16]{0:T(128)S(1)}, s32[16]{0:T(128)}, u32[]{:S(2)}) copy-start(s32[16]{0:T(128)} %param.31) | copy-start | bytes 196
  83.2 2.7 %copy-start.6 = (bf16[768,768]{0,1:T(8,128)(2,1)S(1)}, bf16[768,768]{0,1:T(8,128)(2,1)}, u32[]{:S(2)}) copy-start(bf16[768,768]{0,1:T(8,128)(2,1)} %copy.36) | copy-start | bytes 3538948
  83.9 2.7 %copy-start.5 = (bf16[768,768]{0,1:T(8,128)(2,1)S(1)}, bf16[768,768]{0,1:T(8,128)(2,1)}, u32[]{:S(2)}) copy-start(bf16[768,768]{0,1:T(8,128)(2,1)} %copy.39) | copy-start | bytes 3538948
  84.4 1.1 copy-start.3
  87.1 1.3 collective-permute-start.4
  88.4 4.9 %collective-permute-start.5 = (bf16[2,2,16,768]{3,2,1,0:T(8,128)(2,1)S(1)}, bf16[2,2,16,768]{3,2,1,0:T(8,128)(2,1)S(1)}, u32[]{:S(2)}, u32[]{:S(2)}) collective-permute-start(bf16[2,2,16,768]{3,2,1,0:T(8,128)(2,1)S(1)} %pad_maximum_fusion.2), channel_id=1, source_target_pairs={{0,2},{1,3},{2,0},{3,1},{4,6},{5,7},{6,4},{7,5},{8,10},{9,11},{10,... | collective-permute-start | bytes 294920 | tf_op jit(solution)/shard_map/ppermute | solution.py:20
  93.4 6.2 %collective-permute-start.6 = (bf16[4,2,16,768]{3,2,1,0:T(8,128)(2,1)S(1)}, bf16[4,2,16,768]{3,2,1,0:T(8,128)(2,1)S(1)}, u32[]{:S(2)}, u32[]{:S(2)}) collective-permute-start(bf16[4,2,16,768]{3,2,1,0:T(8,128)(2,1)S(1)} %pad_maximum_fusion.1), channel_id=1, source_target_pairs={{0,4},{1,5},{2,6},{3,7},{4,0},{5,1},{6,2},{7,3},{8,12},{9,13},{10,... | collective-permute-start | bytes 589832 | tf_op jit(solution)/shard_map/ppermute | solution.py:20
  99.7 18.9 %collective-permute-start.7 = (bf16[8,2,16,768]{3,2,1,0:T(8,128)(2,1)S(1)}, bf16[8,2,16,768]{3,2,1,0:T(8,128)(2,1)S(1)}, u32[]{:S(2)}, u32[]{:S(2)}) collective-permute-start(bf16[8,2,16,768]{3,2,1,0:T(8,128)(2,1)S(1)} %pad_maximum_fusion), channel_id=1, source_target_pairs={{0,8},{1,9},{2,10},{3,11},{4,12},{5,13},{6,14},{7,15},{8,0},{9,1},... | collective-permute-start | bytes 1179656 | tf_op jit(solution)/shard_map/ppermute | solution.py:20
  123.1 10.2 %copy-start.9 = (bf16[256,16,48]{2,1,0:T(8,128)(2,1)S(1)}, bf16[256,16,48]{2,1,0:T(8,128)(2,1)}, u32[]{:S(2)}) copy-start(bf16[256,16,48]{2,1,0:T(8,128)(2,1)} %reshape_squeeze.14) | copy-start | bytes 1179652
  133.4 7.8 %copy-start.14 = (bf16[768,768]{1,0:T(8,128)(2,1)S(1)}, bf16[768,768]{1,0:T(8,128)(2,1)}, u32[]{:S(2)}) copy-start(bf16[768,768]{1,0:T(8,128)(2,1)} %param.29) | copy-start | bytes 3538948
  141.1 2.6 %copy-start.1 = (bf16[768,768]{1,0:T(8,128)(2,1)S(1)}, bf16[768,768]{1,0:T(8,128)(2,1)}, u32[]{:S(2)}) copy-start(bf16[768,768]{1,0:T(8,128)(2,1)} %param.21) | copy-start | bytes 3538948
